TPU v7x, 128 devices: a whole 4x4x4 slice. The times are simulated.
128 devices in a mesh: mem: 4 (over z_lo, core), wide: 32 (over x, z_hi, y).
Axes of the slice: x: 4, y: 4, z: 4 (z_hi: 2, z_lo: 2; z = z_hi * 2 + z_lo), core: 2. Of those that a mesh axis runs over, the one named last changes fastest.
Arguments:
- control: float32 [8, 64, 128, 720], P('mem', 'wide'), may hold values from -6 to 6
- perturb: float32 [8, 3, 64, 128, 720], P('mem', None, None, 'wide'), may hold values from -6 to 6
- obs_count: int32 [128, 720], P('wide'), may hold values from 0 to 3
- obs_kind: int32 [128, 720], P('wide'), may hold values from 0 to 7
- obs_table: float32 [8, 192], replicated, may hold values from 0.25 to 4
- band_filter: float32 [64, 64], replicated, may hold values from -0.9 to 1.2, as said below
- diffusivity: float32 [128, 720], replicated, may hold values from 0.04 to 0.24
Outputs:
- hessian_product: float32 [8, 64, 128, 720], P('mem', 'wide')
Inputs may be any that keep to these rules, and one draw needn't show every extreme that they name: band_filter[i, j] is zero where |i - j| > 4; its diagonal lies between 0.8 and 1.2.
All inputs are finite; a program needn't handle non-finite values.
Results may differ from a plain program's by a relative error of at most 0.00005.
Values sent between devices are 32-bit elements; how exact they have to be, the bound alone decides.
No kernel may reach another device: no remote copies, remote signals or barrier semaphores. Data moves between devices by JAX's collectives and lax.ppermute only.
A program may use at most 64 MiB of HBM per device.

v0:
```python
import functools

import jax
import jax.numpy as jnp
from jax import lax
from jax.experimental import pallas as pl
from jax.experimental.pallas import tpu as pltpu
from jax.sharding import PartitionSpec as P


ITERS = 16
SUB = 8
LANES = 128
VMEM = pl.BlockSpec(memory_space=pltpu.VMEM)
SMEM = pl.BlockSpec(memory_space=pltpu.SMEM)
HBM = pl.BlockSpec(memory_space=pltpu.HBM)
HIGHEST = lax.Precision.HIGHEST


def dot(a, b, contract=((1,), (0,))):
    return lax.dot_general(
        a, b, (contract, ((), ())), precision=HIGHEST, preferred_element_type=jnp.float32
    )


def iota(shape, dim):
    return lax.broadcasted_iota(jnp.int32, shape, dim)


def ones_where(mask):
    return jnp.where(mask, 1.0, 0.0).astype(jnp.float32)


def blocks_of(lon):
    return [(start, min(LANES, lon - start)) for start in range(0, lon, LANES)]


def coefficients(diff_ref, east, north, turned, flat):
    rows, steps = east.shape[:2]
    lon, lat = diff_ref.shape
    blocks = lat // rows
    copies = LANES // blocks
    for start, width in blocks_of(lon):
        turned[start // LANES, :lat, :width] = diff_ref[start : start + width, :].T
    for i in range(rows):
        for start, width in blocks_of(lon):
            picked = turned[start // LANES, pl.ds(i, blocks, stride=rows), :]
            flat[i, start : start + LANES, :] = jnp.concatenate([picked] * copies, 0).T
    edge = lax.rem(iota((SUB, LANES), 1), blocks) == blocks - 1
    first = [flat[i, pl.ds(0, SUB, stride=steps), :] for i in range(rows)]
    here = list(first)
    for r in range(steps):
        for i in range(rows):
            if r + 1 < steps:
                there = flat[i, pl.ds(r + 1, SUB, stride=steps), :]
            else:
                there = pltpu.roll(first[i], SUB - 1, 0)
            east[i, r] = 0.5 * (here[i] + there)
            if i + 1 < rows:
                north[i, r] = 0.5 * (here[i] + here[i + 1])
            else:
                up = 0.5 * (here[i] + pltpu.roll(start_of_row, LANES - 1, 1))
                north[i, r] = jnp.where(edge, jnp.zeros_like(up), up)
            if i == 0:
                start_of_row = here[0]
            here[i] = there if i else here[i]
            if i == 0:
                next_of_row = there
        here[0] = next_of_row


def diffuse_in_place(field, east, north):
    rows, steps = field.shape[:2]

    def one_step(step_index, carry):
        here = [field[i, 0] for i in range(rows)]
        ahead = [pltpu.roll(f, SUB - 1, 0) for f in here]
        before = [
            pltpu.roll(east[i, steps - 1] * (ahead[i] - field[i, steps - 1]), 1, 0)
            for i in range(rows)
        ]
        for r in range(steps):
            there = [field[i, r + 1] if r + 1 < steps else ahead[i] for i in range(rows)]
            up = here[1:] + [pltpu.roll(here[0], LANES - 1, 1)]
            flux_north = [north[i, r] * (up[i] - here[i]) for i in range(rows)]
            down = [pltpu.roll(flux_north[-1], 1, 1)] + flux_north[:-1]
            for i in range(rows):
                flux_east = east[i, r] * (there[i] - here[i])
                field[i, r] = here[i] + ((flux_east - before[i]) + (flux_north[i] - down[i]))
                before[i] = flux_east
            here = there
        return carry

    lax.fori_loop(0, ITERS, one_step, 0)


def spread_out(
    control_hbm, diff_hbm, sent_ref, east_hbm, north_hbm,
    diffusivity, control, east, north, field, turned, flat, sems,
):
    planes, lon, lat = control.shape
    rows, steps = field.shape[:2]
    blocks = lat // rows
    tiles = turned.shape[0]
    fetch_diff = pltpu.make_async_copy(diff_hbm, diffusivity, sems.at[0])
    fetch_diff.start()
    fetch = pltpu.make_async_copy(control_hbm, control, sems.at[1])
    fetch.start()
    turned[tiles - 1] = jnp.zeros(turned.shape[1:], jnp.float32)
    flat[:, (tiles - 1) * LANES :, :] = jnp.zeros((rows, LANES, LANES), jnp.float32)
    fetch_diff.wait()
    coefficients(diffusivity, east, north, turned, flat)
    keep_east = pltpu.make_async_copy(east, east_hbm, sems.at[2])
    keep_north = pltpu.make_async_copy(north, north_hbm, sems.at[3])
    keep_east.start()
    keep_north.start()
    fetch.wait()
    for q in range(planes):
        for start, width in blocks_of(lon):
            turned[start // LANES, lat * q : lat * q + lat, :width] = control[
                q, start : start + width, :
            ].T
    for i in range(rows):
        for start, width in blocks_of(lon):
            picked = [
                turned[start // LANES, pl.ds(lat * q + i, blocks, stride=rows), :]
                for q in range(planes)
            ]
            flat[i, start : start + LANES, :] = jnp.concatenate(picked, 0).T
        for r in range(steps):
            field[i, r] = flat[i, pl.ds(r, SUB, stride=steps), :]
    diffuse_in_place(field, east, north)
    for i in range(rows):
        for r in range(steps):
            flat[i, pl.ds(r, SUB, stride=steps), :] = field[i, r]
        for start, width in blocks_of(lon):
            block = flat[i, start : start + LANES, :].T
            for q in range(planes):
                row = (start // LANES * planes + q) * rows + i
                sent_ref[pl.ds(row, blocks, stride=tiles * planes * rows), :] = block[
                    q * blocks : (q + 1) * blocks, :
                ]
    keep_east.wait()
    keep_north.wait()


def gather_in(
    a_ref, b_ref, control_hbm, east_hbm, north_hbm, out_hbm,
    control, east, north, field, turned, flat, sems,
):
    planes, lon, lat = control.shape
    rows, steps = field.shape[:2]
    blocks = lat // rows
    tiles_a = a_ref.shape[0] // (blocks * planes * rows)
    tiles_b = b_ref.shape[0] // (blocks * planes * rows)
    fetches = [
        pltpu.make_async_copy(source, target, sems.at[planes + n])
        for n, (source, target) in enumerate(
            ((east_hbm, east), (north_hbm, north), (control_hbm, control))
        )
    ]
    for fetch in fetches:
        fetch.start()
    for i in range(rows):
        for start, width in blocks_of(lon):
            in_ref, tile, tiles = a_ref, start // LANES, tiles_a
            if tile >= tiles_a:
                in_ref, tile, tiles = b_ref, tile - tiles_a, tiles_b
            picked = [
                in_ref[
                    pl.ds((tile * planes + q) * rows + i, blocks, stride=tiles * planes * rows), :
                ]
                for q in range(planes)
            ]
            flat[i, start : start + LANES, :] = jnp.concatenate(picked, 0).T
        for r in range(steps):
            field[i, r] = flat[i, pl.ds(r, SUB, stride=steps), :]
    fetches[0].wait()
    fetches[1].wait()
    diffuse_in_place(field, east, north)
    for i in range(rows):
        for r in range(steps):
            flat[i, pl.ds(r, SUB, stride=steps), :] = field[i, r]
        for start, width in blocks_of(lon):
            block = flat[i, start : start + LANES, :].T
            for q in range(planes):
                turned[start // LANES, pl.ds(lat * q + i, blocks, stride=rows), :] = block[
                    q * blocks : (q + 1) * blocks, :
                ]
    fetches[2].wait()
    stores = []
    for q in range(planes):
        for start, width in blocks_of(lon):
            back = turned[start // LANES, lat * q : lat * q + lat, :].T
            place = pl.ds(start, width)
            control[q, place, :] = control[q, place, :] + back[:width, :]
        stores.append(pltpu.make_async_copy(control.at[q], out_hbm.at[q], sems.at[q]))
        stores[-1].start()
    for store in stores:
        store.wait()


def prepare(core_ref, filter_ref, table_ref, count_ref, kind_ref, band_ref, band_t_ref, *weight_refs):
    levels = filter_ref.shape[0]
    flat = band_ref.shape[0]
    rows = flat // levels
    kinds, columns = table_ref.shape
    lon = count_ref.shape[1]
    own = weight_refs[0].shape[0]
    variables = columns // levels
    share = own // variables // rows
    spread = ones_where(iota((flat, levels), 0) // rows == iota((flat, levels), 1))
    spread_t = ones_where(iota((levels, flat), 1) // rows == iota((levels, flat), 0))
    same = lax.rem(iota((flat, flat), 0), rows) == lax.rem(iota((flat, flat), 1), rows)
    weight = filter_ref[...]
    band_ref[...] = jnp.where(same, dot(dot(spread, weight), spread_t), 0.0)
    band_t_ref[...] = jnp.where(same, dot(dot(spread, weight, ((1,), (1,))), spread_t), 0.0)
    row = iota((own, columns), 0)
    column = (
        row // (share * rows) * levels
        + core_ref[0] * share
        + lax.rem(row // rows, share)
    )
    picked = dot(ones_where(column == iota((own, columns), 1)), table_ref[...], ((1,), (1,)))
    wide = kinds * rows
    each = ones_where(iota((kinds, wide), 1) // rows == iota((kinds, wide), 0))
    match = lax.rem(iota((own, wide), 0), rows) == lax.rem(iota((own, wide), 1), rows)
    table = jnp.where(match, dot(picked, each), 0.0)
    repeat = ones_where(lax.rem(iota((wide, rows), 0), rows) == iota((wide, rows), 1))
    kind = dot(repeat, kind_ref[...].astype(jnp.float32))
    count = dot(repeat, count_ref[...].astype(jnp.float32))
    which = (iota((wide, lon), 0) // rows).astype(jnp.float32)
    chosen = jnp.where(kind == which, count, 0.0)
    start = 0
    for weight_ref in weight_refs[:-1]:
        width = weight_ref.shape[1]
        weight_ref[...] = dot(table, chosen[:, start : start + width])
        start += width
    tail = jnp.concatenate(
        [chosen[:, start:], jnp.zeros((wide, start + LANES - lon), jnp.float32)], 1
    )
    weight_refs[-1][...] = dot(table, tail).T[: lon - start, :]


def rows_of(perturb_ref, out_ref):
    levels, rows, lon = perturb_ref.shape
    pair = SUB // rows
    for tile, (start, width) in enumerate(blocks_of(lon)):
        if width < LANES:
            out_ref[tile] = jnp.zeros(out_ref.shape[1:], jnp.float32)
        for t in range(levels // pair):
            out_ref[tile, SUB * t : SUB * t + SUB, :width] = jnp.concatenate(
                [perturb_ref[pair * t + u, :, start : start + width] for u in range(pair)], 0
            )


def fetch_tiles(first, perturb_hbm, perturb, sems):
    copies = [
        pltpu.make_async_copy(perturb_hbm.at[first + u], perturb.at[u], sems.at[u])
        for u in range(perturb.shape[0])
    ]
    for copy in copies:
        copy.start()
    return copies


def partial_sums(
    first, core_ref, band_ref, pieces_ref, perturb_hbm, send_ref, keep_ref,
    perturb, filtered, parts, sems,
):
    count, products, flat = perturb.shape[:3]
    members = filtered.shape[1] // LANES
    variables = products // members
    piece = pieces_ref.shape[2] // members
    core = core_ref[0]
    half = flat // 2
    copies = fetch_tiles(first, perturb_hbm, perturb, sems)
    for u in range(count):
        mine = [
            pieces_ref[:, first + u, piece * k : piece * k + piece, :].reshape(flat, LANES)
            for k in range(members)
        ]
        filtered[...] = dot(band_ref[...], jnp.concatenate(mine, 1))
        copies[u].wait()
        for side, out_ref in enumerate((send_ref, keep_ref)):
            base = (core if side else 1 - core) * half
            turned = out_ref.shape[0] < variables * half
            to_ref = parts.at[side] if turned else out_ref
            for t in range(half // SUB):
                at = pl.ds(pl.multiple_of(base + t * SUB, SUB), SUB)
                fields = [filtered[at, LANES * k : LANES * (k + 1)] for k in range(members)]
                for v in range(variables):
                    total = perturb[u, v, at, :] * fields[0]
                    for k in range(1, members):
                        total = total + perturb[u, k * variables + v, at, :] * fields[k]
                    row = v * half + t * SUB
                    to_ref[row : row + SUB, u * LANES : (u + 1) * LANES] = total
            if turned:
                for v in range(variables):
                    block = parts[side, v * half : (v + 1) * half, :].T
                    out_ref[:, v * half : (v + 1) * half] = block[: out_ref.shape[0], :]


def lift(first, place, core_ref, band_ref, own_ref, other_ref, perturb_hbm, *rest):
    out_ref, perturb, adjoint, parts, sems = rest[-5:]
    count, products, flat = perturb.shape[:3]
    members = adjoint.shape[1] // LANES
    variables = products // members
    piece = out_ref.shape[2] // members
    core = core_ref[0]
    half = flat // 2
    copies = fetch_tiles(first, perturb_hbm, perturb, sems)
    for earlier_ref in rest[:-5]:
        out_ref[:, :place] = earlier_ref[...]
    sides = [own_ref, other_ref]
    if own_ref.shape[0] < variables * half:
        empty = jnp.zeros((LANES - own_ref.shape[0], half), jnp.float32)
        for side, weighted in enumerate(sides):
            for v in range(variables):
                block = jnp.concatenate([weighted[:, v * half : (v + 1) * half], empty], 0)
                parts[side, v * half : (v + 1) * half, :] = block.T
        sides = [parts.at[0], parts.at[1]]
    for u in range(count):
        copies[u].wait()
        for side, weighted in enumerate(sides):
            base = (core if side == 0 else 1 - core) * half
            for t in range(half // SUB):
                at = pl.ds(pl.multiple_of(base + t * SUB, SUB), SUB)
                terms = []
                for v in range(variables):
                    row = v * half + t * SUB
                    terms.append(weighted[row : row + SUB, u * LANES : (u + 1) * LANES])
                for k in range(members):
                    total = perturb[u, k * variables, at, :] * terms[0]
                    for v in range(1, variables):
                        total = total + perturb[u, k * variables + v, at, :] * terms[v]
                    adjoint[at, LANES * k : LANES * (k + 1)] = total
        whole = dot(band_ref[...], adjoint[...])
        for k in range(members):
            out_ref[:, place + u, piece * k : piece * k + piece, :] = whole[
                :, LANES * k : LANES * (k + 1)
            ].reshape(-1, piece, LANES)


def add_up(keep_ref, got_ref, out_ref):
    out_ref[...] = keep_ref[...] + got_ref[...]


def weigh(weight_ref, on_chip_ref, got_ref, out_ref):
    out_ref[...] = weight_ref[...] * (on_chip_ref[...] + got_ref[...])


def call(kernel, out_shape, flops, moved, ins=None, outs=None, scratch=(), limit=8, **grid):
    def run(*args):
        return pl.pallas_call(
            kernel,
            out_shape=out_shape,
            in_specs=ins or [VMEM] * len(args),
            out_specs=outs or jax.tree.map(lambda _: VMEM, out_shape),
            scratch_shapes=scratch,
            cost_estimate=pl.CostEstimate(flops=flops, bytes_accessed=moved, transcendentals=0),
            compiler_params=pltpu.CompilerParams(vmem_limit_bytes=limit << 20),
            **grid,
        )(*args)

    return run


def f32(*shape):
    return jax.ShapeDtypeStruct(shape, jnp.float32)


def local(control, perturb, obs_count, obs_kind, obs_table, band_filter, diffusivity):
    members, level_planes, lat, lon = control.shape
    variables, levels, rows = perturb.shape[1:4]
    devices = lax.axis_size("wide")
    planes = members * level_planes
    steps = lon // SUB
    flat = levels * rows
    half = flat // 2
    tiles = -(-lon // LANES)
    chunks = [(0, 2), (2, tiles - 3), (tiles - 1, 1)]
    groups = [(0, 2), (2, tiles - 2), (2, tiles - 2)]
    height = planes * rows
    control_t = jnp.swapaxes(control, 2, 3).reshape(planes, lon, lat)
    control_t = pltpu.with_memory_space_constraint(control_t, pltpu.HBM)
    diff_t = jnp.swapaxes(diffusivity, 0, 1)
    core = (lax.axis_index("mem") % 2).astype(jnp.int32).reshape(1)

    coefs = f32(rows, steps, SUB, LANES)
    vmem = [
        (planes, lon, lat),
        coefs.shape,
        coefs.shape,
        coefs.shape,
        (tiles, planes * lat, LANES),
        (rows, tiles * LANES, LANES),
    ]
    vmem = [pltpu.VMEM(shape, jnp.float32) for shape in vmem]
    resting = pltpu.HBM(coefs.shape, jnp.float32)
    work = planes * lat * lon * ITERS * 8
    size = planes * lat * lon * 4

    sent, east, north = call(
        spread_out,
        [f32(devices * tiles * height, LANES), resting, resting],
        work,
        2 * size,
        [HBM, HBM],
        [VMEM, HBM, HBM],
        [pltpu.VMEM((lon, lat), jnp.float32), *vmem, pltpu.SemaphoreType.DMA((4,))],
        20,
    )(control_t, pltpu.with_memory_space_constraint(diff_t, pltpu.HBM))
    east, north = (pltpu.with_memory_space_constraint(e, pltpu.HBM) for e in (east, north))

    def exchange(sent):
        return lax.all_to_all(sent.reshape(devices, -1, height, LANES), "wide", 0, 0, tiled=True)

    pieces = exchange(sent)

    used = lon - (tiles - 1) * LANES
    parts = [f32(variables * half, count * LANES) for first, count in chunks[:-1]]
    parts.append(f32(used, variables * half))
    band, band_t, *weights = call(
        prepare,
        [f32(flat, flat), f32(flat, flat)] + parts,
        1 << 28,
        4 << 20,
        [SMEM] + [VMEM] * 4,
    )(core, band_filter, obs_table, obs_count, obs_kind)
    perturb = perturb.reshape(members * variables, levels, rows, lon)
    perturb = call(
        rows_of,
        f32(tiles, members * variables, flat, LANES),
        1 << 20,
        6 * size,
        [pl.BlockSpec((None, levels, rows, lon), lambda g: (g, 0, 0, 0))],
        pl.BlockSpec((tiles, None, flat, LANES), lambda g: (0, g, 0, 0)),
        grid=(members * variables,),
    )(pltpu.with_memory_space_constraint(perturb, pltpu.HBM))
    perturb = pltpu.with_memory_space_constraint(perturb, pltpu.HBM)

    other_core = [(i, i ^ 1) for i in range(4)]
    next_chip = [(i, i ^ 2) for i in range(4)]
    home = None
    lifted = []
    for h, (first, count) in enumerate(chunks):
        part = parts[h]
        scratch = [
            pltpu.VMEM((count, members * variables, flat, LANES), jnp.float32),
            pltpu.VMEM((flat, members * LANES), jnp.float32),
            pltpu.VMEM((2, variables * half, LANES), jnp.float32),
            pltpu.SemaphoreType.DMA((count,)),
        ]
        send, keep = call(
            functools.partial(partial_sums, first),
            [part, part],
            count << 28,
            count * size,
            [SMEM, VMEM, VMEM, HBM],
            None,
            scratch,
        )(core, band, pieces, perturb)
        got = lax.ppermute(send, "mem", other_core)
        on_chip = call(add_up, part, 1 << 18, size)(keep, got)
        got = lax.ppermute(on_chip, "mem", next_chip)
        own = call(weigh, part, 1 << 18, size)(weights[h], on_chip, got)
        other = lax.ppermute(own, "mem", other_core)
        start, total = groups[h]
        place = first - start
        begins = place == 0

        home = call(
            functools.partial(lift, first, place),
            f32(devices, place + count, height, LANES),
            count << 28,
            count * size,
            [SMEM, VMEM, VMEM, VMEM, HBM] + ([] if begins else [VMEM]),
            None,
            scratch,
        )(core, band_t, own, other, perturb, *([] if begins else [home]))
        if first + count == start + total:
            lifted.append(exchange(home).reshape(-1, LANES))

    out = call(
        gather_in,
        pltpu.HBM((planes, lon, lat), jnp.float32),
        work,
        3 * size,
        [VMEM, VMEM, HBM, HBM, HBM],
        HBM,
        [*vmem, pltpu.SemaphoreType.DMA((planes + 3,))],
        20,
    )(*lifted, control_t, east, north)
    return jnp.swapaxes(out.reshape(members, level_planes, lon, lat), 2, 3)


def solution(mesh):
    placed = (
        P("mem", "wide", None, None),
        P("mem", None, None, "wide", None),
        P("wide", None),
        P("wide", None),
        P(),
        P(),
        P(),
    )

    return jax.shard_map(
        local, mesh=mesh, in_specs=placed, out_specs=P("mem", "wide", None, None), check_vma=False
    )
```

profile of v0, /device:TPU:0, one launch (start us, length us, event | category | flops | bytes accessed | tf_op | source)
XLA Modules:
  0.0 141.8 jit_solution(2316286643894638520)
XLA Ops:
  0.0 12.4 %shard_map.74 = (f32[3072,128]{1,0:T(8,128)}, f32[4,90,8,128]{3,2,1,0:T(8,128)}, f32[4,90,8,128]{3,2,1,0:T(8,128)}) custom-call(f32[4,720,128]{2,1,0:T(8,128)} %bitcast.14, f32[720,128]{1,0:T(8,128)} %bitcast.17), custom_call_target="tpu_custom_call" | custom-call | flops 47185920 | bytes 2949120 | tf_op jit(solution)/shard_map/pallas_call | solution.py:355
  12.4 10.8 %all-to-all-start = ((f32[32,6,16,128]{3,2,1,0:T(8,128)}), f32[32,6,16,128]{3,2,1,0:T(8,128)S(1)}, u32[]{:S(2)}, u32[]{:S(2)}) async-start(f32[32,6,16,128]{3,2,1,0:T(8,128)} %bitcast.4), calls=%async_computation | async-start | bytes 3145728 | tf_op jit(solution)/shard_map/all_to_all | solution.py:417
  23.2 0.0 copy-start.4
  23.2 0.0 copy-start.5
  23.2 0.0 copy-start.6
  23.2 0.0 copy-start.7
  23.3 4.3 %shard_map.75.perturb_hbm = f32[6,6,256,128]{3,2,1,0:T(8,128)S(1)} custom-call(f32[6,64,4,720]{3,2,1,0:T(4,128)} %bitcast.16), custom_call_target="tpu_custom_call" | custom-call | flops 1048576 | bytes 8847360 | tf_op jit(solution)/shard_map/pallas_call | solution.py:355
  27.5 0.0 copy-start
  27.5 2.1 %copy-done = f32[6,6,256,128]{3,2,1,0:T(8,128)} copy-done((f32[6,6,256,128]{3,2,1,0:T(8,128)}, f32[6,6,256,128]{3,2,1,0:T(8,128)S(1)}, u32[]{:S(2)}) %copy-start) | copy-done | bytes 4718616
  29.7 0.0 copy-done.4
  29.7 0.0 copy-done.5
  29.7 0.0 copy-done.6
  29.7 0.0 copy-done.7
  29.7 3.0 %shard_map.73 = (f32[256,256]{1,0:T(8,128)S(1)}, f32[256,256]{1,0:T(8,128)S(1)}, f32[384,256]{1,0:T(8,128)S(1)}, f32[384,384]{1,0:T(8,128)S(1)}, f32[80,384]{1,0:T(8,128)S(1)}) custom-call(s32[1]{0:T(128)} %bitcast.core_ref, f32[64,64]{1,0:T(8,128)S(1)} %copy-done.4, f32[8,192]{1,0:T(8,128)S(1)} %copy-done.7, s32[4,720]{1,0:T(4,128)S(1)} %copy-done.5, ...), custom_call_target="tpu_custom_call" | custom-call | flops 268435456 | bytes 4194304 | tf_op jit(solution)/shard_map/pallas_call | solution.py:355
  32.7 0.0 copy-start.2
  32.7 0.7 copy-done.2
  33.5 13.2 %all-to-all-done.pieces_ref = f32[32,6,16,128]{3,2,1,0:T(8,128)S(1)} async-done(((f32[32,6,16,128]{3,2,1,0:T(8,128)}), f32[32,6,16,128]{3,2,1,0:T(8,128)S(1)}, u32[]{:S(2)}, u32[]{:S(2)}) %all-to-all-start) | async-done | bytes 1572896 | tf_op jit(solution)/shard_map/all_to_all | solution.py:417
  46.6 2.5 %shard_map.83 = (f32[384,384]{1,0:T(8,128)S(1)}, f32[384,384]{1,0:T(8,128)S(1)}) custom-call(s32[1]{0:T(128)} %bitcast.core_ref, f32[256,256]{1,0:T(8,128)S(1)} %get-tuple-element.21.band_ref, f32[32,6,16,128]{3,2,1,0:T(8,128)S(1)} %all-to-all-done.pieces_ref, f32[6,6,256,128]{3,2,1,0:T(8,128)} %copy-done), custom_call_target="tpu_custom_call" | custom-call | flops 805306368 | bytes 4423680 | tf_op jit(solution)/shard_map/pallas_call | solution.py:355
  49.1 0.1 collective-permute-start.6
  49.2 1.8 %shard_map.76 = (f32[384,256]{1,0:T(8,128)S(1)}, f32[384,256]{1,0:T(8,128)S(1)}) custom-call(s32[1]{0:T(128)} %bitcast.core_ref, f32[256,256]{1,0:T(8,128)S(1)} %get-tuple-element.21.band_ref, f32[32,6,16,128]{3,2,1,0:T(8,128)S(1)} %all-to-all-done.pieces_ref, f32[6,6,256,128]{3,2,1,0:T(8,128)} %copy-done), custom_call_target="tpu_custom_call" | custom-call | flops 536870912 | bytes 2949120 | tf_op jit(solution)/shard_map/pallas_call | solution.py:355
  51.0 0.0 copy-start.3
  51.1 0.6 collective-permute-start
  51.6 1.3 collective-permute-done.got_ref
  53.0 1.1 collective-permute-start.1
  54.1 0.0 collective-permute-done.6.got_ref
  54.1 0.1 shard_map.84.on_chip_ref
  54.2 1.1 collective-permute-start.7
  55.3 9.8 %collective-permute-done.1.got_ref = f32[384,256]{1,0:T(8,128)S(1)} collective-permute-done((f32[384,256]{1,0:T(8,128)S(1)}, f32[384,256]{1,0:T(8,128)S(1)}, u32[]{:S(2)}, u32[]{:S(2)}) %collective-permute-start.1) | collective-permute-done | bytes 393248 | tf_op jit(solution)/shard_map/ppermute | solution.py:466
  65.1 0.0 copy-done.3
  65.1 0.1 shard_map.78.own_ref
  65.2 0.1 collective-permute-start.2
  65.2 11.9 %collective-permute-done.7.got_ref = f32[384,384]{1,0:T(8,128)S(1)} collective-permute-done((f32[384,384]{1,0:T(8,128)S(1)}, f32[384,384]{1,0:T(8,128)S(1)}, u32[]{:S(2)}, u32[]{:S(2)}) %collective-permute-start.7) | collective-permute-done | bytes 589856 | tf_op jit(solution)/shard_map/ppermute | solution.py:466
  77.1 0.1 shard_map.85.own_ref
  77.2 0.1 collective-permute-start.8
  77.3 0.0 collective-permute-done.2.other_ref
  77.3 2.4 %shard_map.79 = f32[32,2,16,128]{3,2,1,0:T(8,128)S(1)} custom-call(s32[1]{0:T(128)} %bitcast.core_ref, f32[256,256]{1,0:T(8,128)S(1)} %get-tuple-element.19.band_ref, f32[384,256]{1,0:T(8,128)S(1)} %shard_map.78.own_ref, f32[384,256]{1,0:T(8,128)S(1)} %collective-permute-done.2.other_ref, f32[6,6,256,128]{3,2,1,0:T(8,128)} %copy-done), custom_call_target="tpu_custom_call" | custom-call | flops 536870912 | bytes 2949120 | tf_op jit(solution)/shard_map/pallas_call | solution.py:355
  79.7 0.0 copy-start.1
  79.8 0.8 copy-done.1
  80.5 5.5 %all-to-all-start.1 = ((f32[32,2,16,128]{3,2,1,0:T(8,128)}), f32[32,2,16,128]{3,2,1,0:T(8,128)S(1)}, u32[]{:S(2)}, u32[]{:S(2)}) async-start(f32[32,2,16,128]{3,2,1,0:T(8,128)} %copy-done.1), calls=%async_computation.1 | async-start | bytes 1048576 | tf_op jit(solution)/shard_map/all_to_all | solution.py:417
  86.0 1.4 %shard_map.80 = (f32[80,384]{1,0:T(8,128)S(1)}, f32[80,384]{1,0:T(8,128)S(1)}) custom-call(s32[1]{0:T(128)} %bitcast.core_ref, f32[256,256]{1,0:T(8,128)S(1)} %get-tuple-element.21.band_ref, f32[32,6,16,128]{3,2,1,0:T(8,128)S(1)} %all-to-all-done.pieces_ref, f32[6,6,256,128]{3,2,1,0:T(8,128)} %copy-done), custom_call_target="tpu_custom_call" | custom-call | flops 268435456 | bytes 1474560 | tf_op jit(solution)/shard_map/pallas_call | solution.py:355
  87.5 0.3 collective-permute-start.3
  87.7 1.1 collective-permute-done.3.got_ref
  88.9 1.1 collective-permute-start.4
  90.0 8.0 %collective-permute-done.4.got_ref = f32[80,384]{1,0:T(8,128)S(1)} collective-permute-done((f32[80,384]{1,0:T(8,128)S(1)}, f32[80,384]{1,0:T(8,128)S(1)}, u32[]{:S(2)}, u32[]{:S(2)}) %collective-permute-start.4) | collective-permute-done | bytes 122912 | tf_op jit(solution)/shard_map/ppermute | solution.py:466
  98.0 0.1 collective-permute-start.5
  98.1 0.0 collective-permute-done.8.other_ref
  98.1 3.9 %shard_map.86.rest_0_ = f32[32,3,16,128]{3,2,1,0:T(8,128)S(1)} custom-call(s32[1]{0:T(128)} %bitcast.core_ref, f32[256,256]{1,0:T(8,128)S(1)} %get-tuple-element.19.band_ref, f32[384,384]{1,0:T(8,128)S(1)} %shard_map.85.own_ref, f32[384,384]{1,0:T(8,128)} %collective-permute-done.8.other_ref, f32[6,6,256,128]{3,2,1,0:T(8,128)} %copy-done), custom_call_target="tpu_custom_call" | custom-call | flops 805306368 | bytes 4423680 | tf_op jit(solution)/shard_map/pallas_call | solution.py:355
  102.1 0.0 collective-permute-done.5.other_ref
  102.1 1.6 %shard_map.87 = f32[32,4,16,128]{3,2,1,0:T(8,128)S(1)} custom-call(s32[1]{0:T(128)} %bitcast.core_ref, f32[256,256]{1,0:T(8,128)S(1)} %get-tuple-element.19.band_ref, f32[80,384]{1,0:T(8,128)S(1)} %shard_map.82.own_ref, f32[80,384]{1,0:T(8,128)S(1)} %collective-permute-done.5.other_ref, f32[6,6,256,128]{3,2,1,0:T(8,128)} %copy-done, ...), custom_call_target="tpu_custom_call" | custom-call | flops 268435456 | bytes 1474560 | tf_op jit(solution)/shard_map/pallas_call | solution.py:355
  103.7 0.0 all-to-all-done.1
  103.7 26.5 %all_to_all.15 = f32[32,4,16,128]{3,2,1,0:T(8,128)S(1)} all-to-all(f32[32,4,16,128]{3,2,1,0:T(8,128)S(1)} %shard_map.87), channel_id=1, replica_groups=mesh['mem'=4,'wide'=32] {'wide'}, dimensions={0} | all-to-all | bytes 2097152 | tf_op jit(solution)/shard_map/all_to_all | solution.py:417
  130.1 11.5 %shard_map.88 = f32[4,720,128]{2,1,0:T(8,128)} custom-call(f32[1024,128]{1,0:T(8,128)S(1)} %bitcast.13, f32[2048,128]{1,0:T(8,128)S(1)} %bitcast.12, f32[4,720,128]{2,1,0:T(8,128)} %bitcast.15, f32[4,90,8,128]{3,2,1,0:T(8,128)} %get-tuple-element.31.east_hbm, f32[4,90,8,128]{3,2,1,0:T(8,128)} %get-tuple-element.32.north_hbm), custom_call_target="tpu_custom_call" | custom-call | flops 47185920 | bytes 4423680 | tf_op jit(solution)/shard_map/pallas_call | solution.py:355
  (3 shorter events, 0.1 us)
Async XLA Ops:
  12.4 34.2 %all-to-all-start = ((f32[32,6,16,128]{3,2,1,0:T(8,128)}), f32[32,6,16,128]{3,2,1,0:T(8,128)S(1)}, u32[]{:S(2)}, u32[]{:S(2)}) async-start(f32[32,6,16,128]{3,2,1,0:T(8,128)} %bitcast.4), calls=%async_computation | async-start | bytes 3145728 | tf_op jit(solution)/shard_map/all_to_all | solution.py:417
  23.2 6.5 %copy-start.4 = (f32[64,64]{1,0:T(8,128)S(1)}, f32[64,64]{1,0:T(8,128)}, u32[]{:S(2)}) copy-start(f32[64,64]{1,0:T(8,128)} %filter_ref.1) | copy-start | bytes 49156
  23.2 6.4 %copy-start.5 = (s32[4,720]{1,0:T(4,128)S(1)}, s32[4,720]{1,0:T(4,128)}, u32[]{:S(2)}) copy-start(s32[4,720]{1,0:T(4,128)} %count_ref.1) | copy-start | bytes 34564
  23.2 6.4 %copy-start.6 = (s32[4,720]{1,0:T(4,128)S(1)}, s32[4,720]{1,0:T(4,128)}, u32[]{:S(2)}) copy-start(s32[4,720]{1,0:T(4,128)} %kind_ref.1) | copy-start | bytes 34564
  23.2 6.4 %copy-start.7 = (f32[8,192]{1,0:T(8,128)S(1)}, f32[8,192]{1,0:T(8,128)}, u32[]{:S(2)}) copy-start(f32[8,192]{1,0:T(8,128)} %table_ref.1) | copy-start | bytes 18436
  27.5 2.1 %copy-start = (f32[6,6,256,128]{3,2,1,0:T(8,128)}, f32[6,6,256,128]{3,2,1,0:T(8,128)S(1)}, u32[]{:S(2)}) copy-start(f32[6,6,256,128]{3,2,1,0:T(8,128)S(1)} %shard_map.75.perturb_hbm) | copy-start | bytes 14155780
  32.7 0.8 copy-start.2
  49.1 5.0 %collective-permute-start.6 = (f32[384,384]{1,0:T(8,128)S(1)}, f32[384,384]{1,0:T(8,128)S(1)}, u32[]{:S(2)}, u32[]{:S(2)}) collective-permute-start(f32[384,384]{1,0:T(8,128)S(1)} %get-tuple-element.30), channel_id=1, source_target_pairs={{0,32},{32,0},{64,96},{96,64},{1,33},{33,1},{65,97},{97,65},{2,34}... | collective-permute-start | bytes 1769480 | tf_op jit(solution)/shard_map/ppermute | solution.py:464
  51.0 14.0 %copy-start.3 = (f32[384,256]{1,0:T(8,128)S(1)}, f32[384,256]{1,0:T(8,128)}, u32[]{:S(2)}) copy-start(f32[384,256]{1,0:T(8,128)} %copy-done.2) | copy-start | bytes 1179652
  51.1 1.9 %collective-permute-start = (f32[384,256]{1,0:T(8,128)S(1)}, f32[384,256]{1,0:T(8,128)S(1)}, u32[]{:S(2)}, u32[]{:S(2)}) collective-permute-start(f32[384,256]{1,0:T(8,128)S(1)} %get-tuple-element.24), channel_id=1, source_target_pairs={{0,32},{32,0},{64,96},{96,64},{1,33},{33,1},{65,97},{97,65},{2,34}... | collective-permute-start | bytes 1179656 | tf_op jit(solution)/shard_map/ppermute | solution.py:464
  53.0 12.1 %collective-permute-start.1 = (f32[384,256]{1,0:T(8,128)S(1)}, f32[384,256]{1,0:T(8,128)S(1)}, u32[]{:S(2)}, u32[]{:S(2)}) collective-permute-start(f32[384,256]{1,0:T(8,128)S(1)} %shard_map.77.on_chip_ref), channel_id=1, source_target_pairs={{0,64},{32,96},{64,0},{96,32},{1,65},{33,97},{65,1},{97,33},{2,66}... | collective-permute-start | bytes 1179656 | tf_op jit(solution)/shard_map/ppermute | solution.py:466
  54.2 22.9 %collective-permute-start.7 = (f32[384,384]{1,0:T(8,128)S(1)}, f32[384,384]{1,0:T(8,128)S(1)}, u32[]{:S(2)}, u32[]{:S(2)}) collective-permute-start(f32[384,384]{1,0:T(8,128)S(1)} %shard_map.84.on_chip_ref), channel_id=1, source_target_pairs={{0,64},{32,96},{64,0},{96,32},{1,65},{33,97},{65,1},{97,33},{2,66}... | collective-permute-start | bytes 1769480 | tf_op jit(solution)/shard_map/ppermute | solution.py:466
  65.2 12.2 %collective-permute-start.2 = (f32[384,256]{1,0:T(8,128)S(1)}, f32[384,256]{1,0:T(8,128)S(1)}, u32[]{:S(2)}, u32[]{:S(2)}) collective-permute-start(f32[384,256]{1,0:T(8,128)S(1)} %shard_map.78.own_ref), channel_id=1, source_target_pairs={{0,32},{32,0},{64,96},{96,64},{1,33},{33,1},{65,97},{97,65},{2,34}... | collective-permute-start | bytes 1179656 | tf_op jit(solution)/shard_map/ppermute | solution.py:468
  77.2 20.9 %collective-permute-start.8 = (f32[384,384]{1,0:T(8,128)S(1)}, f32[384,384]{1,0:T(8,128)}, u32[]{:S(2)}, u32[]{:S(2)}) collective-permute-start(f32[384,384]{1,0:T(8,128)S(1)} %shard_map.85.own_ref), channel_id=1, source_target_pairs={{0,32},{32,0},{64,96},{96,64},{1,33},{33,1},{65,97},{97,65},{2,34}... | collective-permute-start | bytes 1769480 | tf_op jit(solution)/shard_map/ppermute | solution.py:468
  79.7 0.8 copy-start.1
  80.5 23.1 %all-to-all-start.1 = ((f32[32,2,16,128]{3,2,1,0:T(8,128)}), f32[32,2,16,128]{3,2,1,0:T(8,128)S(1)}, u32[]{:S(2)}, u32[]{:S(2)}) async-start(f32[32,2,16,128]{3,2,1,0:T(8,128)} %copy-done.1), calls=%async_computation.1 | async-start | bytes 1048576 | tf_op jit(solution)/shard_map/all_to_all | solution.py:417
  87.5 1.4 collective-permute-start.3
  88.9 9.1 %collective-permute-start.4 = (f32[80,384]{1,0:T(8,128)S(1)}, f32[80,384]{1,0:T(8,128)S(1)}, u32[]{:S(2)}, u32[]{:S(2)}) collective-permute-start(f32[80,384]{1,0:T(8,128)S(1)} %shard_map.81.on_chip_ref), channel_id=1, source_target_pairs={{0,64},{32,96},{64,0},{96,32},{1,65},{33,97},{65,1},{97,33},{2,66}... | collective-permute-start | bytes 368648 | tf_op jit(solution)/shard_map/ppermute | solution.py:466
  98.0 4.0 %collective-permute-start.5 = (f32[80,384]{1,0:T(8,128)S(1)}, f32[80,384]{1,0:T(8,128)S(1)}, u32[]{:S(2)}, u32[]{:S(2)}) collective-permute-start(f32[80,384]{1,0:T(8,128)S(1)} %shard_map.82.own_ref), channel_id=1, source_target_pairs={{0,32},{32,0},{64,96},{96,64},{1,33},{33,1},{65,97},{97,65},{2,34}... | collective-permute-start | bytes 368648 | tf_op jit(solution)/shard_map/ppermute | solution.py:468
where the time goes:
time: 143 us; the launch traced here: 142 us
  waiting for transfers between devices  45.4 us (32%)
  Pallas kernels  45.1 us (32%)
  blocking collectives  26.5 us (19%)
  starting transfers between devices  20.7 us (14%)
  local copies, waits for them, and re-layouts  3.7 us (3%)
    pallas_call x16, Pallas kernels, run(): pl.pallas_call(kernel, out_shape=out_shape, in_specs=ins or [VMEM] * len(...  45.1 us
    ppermute x3, waiting for transfers between devices, local(): got = lax.ppermute(on_chip, 'mem', next_chip)  29.7 us
    all_to_all x1, blocking collectives, exchange(): lax.all_to_all(sent.reshape(devices, -1, height, LANES), 'wide', 0, 0, ti...  26.5 us
    all_to_all x2, starting transfers between devices, exchange(): lax.all_to_all(sent.reshape(devices, -1, height, LANES), 'wide', 0, 0, ti...  16.2 us
    all_to_all x2, waiting for transfers between devices, exchange(): lax.all_to_all(sent.reshape(devices, -1, height, LANES), 'wide', 0, 0, ti...  13.2 us
    unnamed x16, local copies, waits for them, and re-layouts  3.7 us
    ppermute x3, starting transfers between devices, local(): got = lax.ppermute(on_chip, 'mem', next_chip)  3.28 us
  transfers between devices with their start and end apart: 11, of which 6 were waited for; matrix products, arithmetic and copies ran while one was open for 0% of the time, Pallas kernels for 13%

commit v1 on v0

--- a/solution.py
+++ b/solution.py
@@ -9,6 +9,7 @@
 
 
 ITERS = 16
+UNROLL = 4
 SUB = 8
 LANES = 128
 VMEM = pl.BlockSpec(memory_space=pltpu.VMEM)
@@ -91,17 +92,19 @@
             here = there
         return carry
 
-    lax.fori_loop(0, ITERS, one_step, 0)
+    lax.fori_loop(0, ITERS, one_step, 0, unroll=UNROLL)
 
 
 def spread_out(
     control_hbm, diff_hbm, sent_ref, east_hbm, north_hbm,
-    diffusivity, control, east, north, field, turned, flat, sems,
+    diffusivity, control, east, north, field, turned, flat, staged, sems,
 ):
     planes, lon, lat = control.shape
     rows, steps = field.shape[:2]
     blocks = lat // rows
     tiles = turned.shape[0]
+    height = tiles * planes * rows
+    pitch = staged.shape[0] // blocks
     fetch_diff = pltpu.make_async_copy(diff_hbm, diffusivity, sems.at[0])
     fetch_diff.start()
     fetch = pltpu.make_async_copy(control_hbm, control, sems.at[1])
@@ -137,22 +140,21 @@
             block = flat[i, start : start + LANES, :].T
             for q in range(planes):
                 row = (start // LANES * planes + q) * rows + i
-                sent_ref[pl.ds(row, blocks, stride=tiles * planes * rows), :] = block[
-                    q * blocks : (q + 1) * blocks, :
-                ]
+                staged[pl.ds(row, blocks, stride=pitch), :] = block[q * blocks : (q + 1) * blocks, :]
+    for b in range(blocks):
+        sent_ref[height * b : height * (b + 1), :] = staged[pitch * b : pitch * b + height, :]
     keep_east.wait()
     keep_north.wait()
 
 
 def gather_in(
     a_ref, b_ref, control_hbm, east_hbm, north_hbm, out_hbm,
-    control, east, north, field, turned, flat, sems,
+    control, east, north, field, turned, flat, staged, sems,
 ):
     planes, lon, lat = control.shape
     rows, steps = field.shape[:2]
     blocks = lat // rows
-    tiles_a = a_ref.shape[0] // (blocks * planes * rows)
-    tiles_b = b_ref.shape[0] // (blocks * planes * rows)
+    pitch = staged.shape[0] // blocks
     fetches = [
         pltpu.make_async_copy(source, target, sems.at[planes + n])
         for n, (source, target) in enumerate(
@@ -161,15 +163,18 @@
     ]
     for fetch in fetches:
         fetch.start()
+    at = 0
+    for in_ref in (a_ref, b_ref):
+        height = in_ref.shape[0] // blocks
+        for b in range(blocks):
+            staged[pitch * b + at : pitch * b + at + height, :] = in_ref[
+                height * b : height * (b + 1), :
+            ]
+        at += height
     for i in range(rows):
         for start, width in blocks_of(lon):
-            in_ref, tile, tiles = a_ref, start // LANES, tiles_a
-            if tile >= tiles_a:
-                in_ref, tile, tiles = b_ref, tile - tiles_a, tiles_b
             picked = [
-                in_ref[
-                    pl.ds((tile * planes + q) * rows + i, blocks, stride=tiles * planes * rows), :
-                ]
+                staged[pl.ds((start // LANES * planes + q) * rows + i, blocks, stride=pitch), :]
                 for q in range(planes)
             ]
             flat[i, start : start + LANES, :] = jnp.concatenate(picked, 0).T
@@ -395,6 +400,7 @@
         coefs.shape,
         (tiles, planes * lat, LANES),
         (rows, tiles * LANES, LANES),
+        (devices * (tiles * height + rows), LANES),
     ]
     vmem = [pltpu.VMEM(shape, jnp.float32) for shape in vmem]
     resting = pltpu.HBM(coefs.shape, jnp.float32)

time: 143 us -> 140 us (0.979)
  Pallas kernels: 45.1 us -> 42.4 us
    pallas_call x16, Pallas kernels: 45.1 us -> 42.4 us  [run(): pl.pallas_call(kernel, out_shape=out_shape, in_specs=ins or [VMEM] * len(...]
where the time goes in v1:
time: 140 us; the launch traced here: 139 us
  waiting for transfers between devices  45.5 us (32%)
  Pallas kernels  42.4 us (30%)
  blocking collectives  26.5 us (19%)
  starting transfers between devices  20.7 us (15%)
  local copies, waits for them, and re-layouts  3.7 us (3%)
    pallas_call x16, Pallas kernels, run(): pl.pallas_call(kernel, out_shape=out_shape, in_specs=ins or [VMEM] * len(...  42.4 us
    ppermute x3, waiting for transfers between devices, local(): got = lax.ppermute(on_chip, 'mem', next_chip)  29.9 us
    all_to_all x1, blocking collectives, exchange(): lax.all_to_all(sent.reshape(devices, -1, height, LANES), 'wide', 0, 0, ti...  26.5 us
    all_to_all x2, starting transfers between devices, exchange(): lax.all_to_all(sent.reshape(devices, -1, height, LANES), 'wide', 0, 0, ti...  16 us
    all_to_all x2, waiting for transfers between devices, exchange(): lax.all_to_all(sent.reshape(devices, -1, height, LANES), 'wide', 0, 0, ti...  13.2 us
    unnamed x16, local copies, waits for them, and re-layouts  3.7 us
    ppermute x3, starting transfers between devices, local(): got = lax.ppermute(on_chip, 'mem', next_chip)  3.28 us
  transfers between devices with their start and end apart: 11, of which 6 were waited for; matrix products, arithmetic and copies ran while one was open for 0% of the time, Pallas kernels for 13%

profile of v1, /device:TPU:0, one launch (start us, length us, event | category | flops | bytes accessed | tf_op | source)
XLA Modules:
  0.0 139.3 jit_solution(11604722928668543102)
XLA Ops:
  0.0 11.0 %shard_map.74 = (f32[3072,128]{1,0:T(8,128)}, f32[4,90,8,128]{3,2,1,0:T(8,128)}, f32[4,90,8,128]{3,2,1,0:T(8,128)}) custom-call(f32[4,720,128]{2,1,0:T(8,128)} %bitcast.14, f32[720,128]{1,0:T(8,128)} %bitcast.17), custom_call_target="tpu_custom_call" | custom-call | flops 47185920 | bytes 2949120 | tf_op jit(solution)/shard_map/pallas_call | solution.py:360
  11.0 10.8 %all-to-all-start = ((f32[32,6,16,128]{3,2,1,0:T(8,128)}), f32[32,6,16,128]{3,2,1,0:T(8,128)S(1)}, u32[]{:S(2)}, u32[]{:S(2)}) async-start(f32[32,6,16,128]{3,2,1,0:T(8,128)} %bitcast.4), calls=%async_computation | async-start | bytes 3145728 | tf_op jit(solution)/shard_map/all_to_all | solution.py:423
  21.8 0.0 copy-start.4
  21.8 0.0 copy-start.5
  21.8 0.0 copy-start.6
  21.8 0.0 copy-start.7
  21.8 4.3 %shard_map.75.perturb_hbm = f32[6,6,256,128]{3,2,1,0:T(8,128)S(1)} custom-call(f32[6,64,4,720]{3,2,1,0:T(4,128)} %bitcast.16), custom_call_target="tpu_custom_call" | custom-call | flops 1048576 | bytes 8847360 | tf_op jit(solution)/shard_map/pallas_call | solution.py:360
  26.1 0.0 copy-start
  26.1 2.1 %copy-done = f32[6,6,256,128]{3,2,1,0:T(8,128)} copy-done((f32[6,6,256,128]{3,2,1,0:T(8,128)}, f32[6,6,256,128]{3,2,1,0:T(8,128)S(1)}, u32[]{:S(2)}) %copy-start) | copy-done | bytes 4718616
  28.2 0.0 copy-done.4
  28.2 0.0 copy-done.5
  28.2 0.0 copy-done.6
  28.2 0.0 copy-done.7
  28.3 3.0 %shard_map.73 = (f32[256,256]{1,0:T(8,128)S(1)}, f32[256,256]{1,0:T(8,128)S(1)}, f32[384,256]{1,0:T(8,128)S(1)}, f32[384,384]{1,0:T(8,128)S(1)}, f32[80,384]{1,0:T(8,128)S(1)}) custom-call(s32[1]{0:T(128)} %bitcast.core_ref, f32[64,64]{1,0:T(8,128)S(1)} %copy-done.4, f32[8,192]{1,0:T(8,128)S(1)} %copy-done.7, s32[4,720]{1,0:T(4,128)S(1)} %copy-done.5, ...), custom_call_target="tpu_custom_call" | custom-call | flops 268435456 | bytes 4194304 | tf_op jit(solution)/shard_map/pallas_call | solution.py:360
  31.3 0.0 copy-start.2
  31.3 0.7 copy-done.2
  32.0 13.2 %all-to-all-done.pieces_ref = f32[32,6,16,128]{3,2,1,0:T(8,128)S(1)} async-done(((f32[32,6,16,128]{3,2,1,0:T(8,128)}), f32[32,6,16,128]{3,2,1,0:T(8,128)S(1)}, u32[]{:S(2)}, u32[]{:S(2)}) %all-to-all-start) | async-done | bytes 1572896 | tf_op jit(solution)/shard_map/all_to_all | solution.py:423
  45.2 2.5 %shard_map.83 = (f32[384,384]{1,0:T(8,128)S(1)}, f32[384,384]{1,0:T(8,128)S(1)}) custom-call(s32[1]{0:T(128)} %bitcast.core_ref, f32[256,256]{1,0:T(8,128)S(1)} %get-tuple-element.21.band_ref, f32[32,6,16,128]{3,2,1,0:T(8,128)S(1)} %all-to-all-done.pieces_ref, f32[6,6,256,128]{3,2,1,0:T(8,128)} %copy-done), custom_call_target="tpu_custom_call" | custom-call | flops 805306368 | bytes 4423680 | tf_op jit(solution)/shard_map/pallas_call | solution.py:360
  47.7 0.1 collective-permute-start.6
  47.8 1.8 %shard_map.76 = (f32[384,256]{1,0:T(8,128)S(1)}, f32[384,256]{1,0:T(8,128)S(1)}) custom-call(s32[1]{0:T(128)} %bitcast.core_ref, f32[256,256]{1,0:T(8,128)S(1)} %get-tuple-element.21.band_ref, f32[32,6,16,128]{3,2,1,0:T(8,128)S(1)} %all-to-all-done.pieces_ref, f32[6,6,256,128]{3,2,1,0:T(8,128)} %copy-done), custom_call_target="tpu_custom_call" | custom-call | flops 536870912 | bytes 2949120 | tf_op jit(solution)/shard_map/pallas_call | solution.py:360
  49.6 0.0 copy-start.3
  49.6 0.6 collective-permute-start
  50.2 1.3 collective-permute-done.got_ref
  51.6 1.1 collective-permute-start.1
  52.7 0.0 collective-permute-done.6.got_ref
  52.7 0.1 shard_map.84.on_chip_ref
  52.8 1.1 collective-permute-start.7
  53.8 9.8 %collective-permute-done.1.got_ref = f32[384,256]{1,0:T(8,128)S(1)} collective-permute-done((f32[384,256]{1,0:T(8,128)S(1)}, f32[384,256]{1,0:T(8,128)S(1)}, u32[]{:S(2)}, u32[]{:S(2)}) %collective-permute-start.1) | collective-permute-done | bytes 393248 | tf_op jit(solution)/shard_map/ppermute | solution.py:472
  63.7 0.0 copy-done.3
  63.7 0.1 shard_map.78.own_ref
  63.7 0.1 collective-permute-start.2
  63.8 11.9 %collective-permute-done.7.got_ref = f32[384,384]{1,0:T(8,128)S(1)} collective-permute-done((f32[384,384]{1,0:T(8,128)S(1)}, f32[384,384]{1,0:T(8,128)S(1)}, u32[]{:S(2)}, u32[]{:S(2)}) %collective-permute-start.7) | collective-permute-done | bytes 589856 | tf_op jit(solution)/shard_map/ppermute | solution.py:472
  75.7 0.1 shard_map.85.own_ref
  75.8 0.3 collective-permute-start.8
  76.1 0.0 collective-permute-done.2.other_ref
  76.1 2.4 %shard_map.79 = f32[32,2,16,128]{3,2,1,0:T(8,128)S(1)} custom-call(s32[1]{0:T(128)} %bitcast.core_ref, f32[256,256]{1,0:T(8,128)S(1)} %get-tuple-element.19.band_ref, f32[384,256]{1,0:T(8,128)S(1)} %shard_map.78.own_ref, f32[384,256]{1,0:T(8,128)S(1)} %collective-permute-done.2.other_ref, f32[6,6,256,128]{3,2,1,0:T(8,128)} %copy-done), custom_call_target="tpu_custom_call" | custom-call | flops 536870912 | bytes 2949120 | tf_op jit(solution)/shard_map/pallas_call | solution.py:360
  78.5 0.0 copy-start.1
  78.5 0.8 copy-done.1
  79.3 5.3 %all-to-all-start.1 = ((f32[32,2,16,128]{3,2,1,0:T(8,128)}), f32[32,2,16,128]{3,2,1,0:T(8,128)S(1)}, u32[]{:S(2)}, u32[]{:S(2)}) async-start(f32[32,2,16,128]{3,2,1,0:T(8,128)} %copy-done.1), calls=%async_computation.1 | async-start | bytes 1048576 | tf_op jit(solution)/shard_map/all_to_all | solution.py:423
  84.6 1.4 %shard_map.80 = (f32[80,384]{1,0:T(8,128)S(1)}, f32[80,384]{1,0:T(8,128)S(1)}) custom-call(s32[1]{0:T(128)} %bitcast.core_ref, f32[256,256]{1,0:T(8,128)S(1)} %get-tuple-element.21.band_ref, f32[32,6,16,128]{3,2,1,0:T(8,128)S(1)} %all-to-all-done.pieces_ref, f32[6,6,256,128]{3,2,1,0:T(8,128)} %copy-done), custom_call_target="tpu_custom_call" | custom-call | flops 268435456 | bytes 1474560 | tf_op jit(solution)/shard_map/pallas_call | solution.py:360
  86.0 0.3 collective-permute-start.3
  86.3 1.1 collective-permute-done.3.got_ref
  87.5 1.1 collective-permute-start.4
  88.6 8.2 %collective-permute-done.4.got_ref = f32[80,384]{1,0:T(8,128)S(1)} collective-permute-done((f32[80,384]{1,0:T(8,128)S(1)}, f32[80,384]{1,0:T(8,128)S(1)}, u32[]{:S(2)}, u32[]{:S(2)}) %collective-permute-start.4) | collective-permute-done | bytes 122912 | tf_op jit(solution)/shard_map/ppermute | solution.py:472
  96.8 0.1 collective-permute-start.5
  96.9 0.0 collective-permute-done.8.other_ref
  96.9 3.9 %shard_map.86.rest_0_ = f32[32,3,16,128]{3,2,1,0:T(8,128)S(1)} custom-call(s32[1]{0:T(128)} %bitcast.core_ref, f32[256,256]{1,0:T(8,128)S(1)} %get-tuple-element.19.band_ref, f32[384,384]{1,0:T(8,128)S(1)} %shard_map.85.own_ref, f32[384,384]{1,0:T(8,128)} %collective-permute-done.8.other_ref, f32[6,6,256,128]{3,2,1,0:T(8,128)} %copy-done), custom_call_target="tpu_custom_call" | custom-call | flops 805306368 | bytes 4423680 | tf_op jit(solution)/shard_map/pallas_call | solution.py:360
  100.8 0.0 collective-permute-done.5.other_ref
  100.8 1.6 %shard_map.87 = f32[32,4,16,128]{3,2,1,0:T(8,128)S(1)} custom-call(s32[1]{0:T(128)} %bitcast.core_ref, f32[256,256]{1,0:T(8,128)S(1)} %get-tuple-element.19.band_ref, f32[80,384]{1,0:T(8,128)S(1)} %shard_map.82.own_ref, f32[80,384]{1,0:T(8,128)S(1)} %collective-permute-done.5.other_ref, f32[6,6,256,128]{3,2,1,0:T(8,128)} %copy-done, ...), custom_call_target="tpu_custom_call" | custom-call | flops 268435456 | bytes 1474560 | tf_op jit(solution)/shard_map/pallas_call | solution.py:360
  102.4 0.0 all-to-all-done.1
  102.4 26.5 %all_to_all.15 = f32[32,4,16,128]{3,2,1,0:T(8,128)S(1)} all-to-all(f32[32,4,16,128]{3,2,1,0:T(8,128)S(1)} %shard_map.87), channel_id=1, replica_groups=mesh['mem'=4,'wide'=32] {'wide'}, dimensions={0} | all-to-all | bytes 2097152 | tf_op jit(solution)/shard_map/all_to_all | solution.py:423
  128.9 10.2 %shard_map.88 = f32[4,720,128]{2,1,0:T(8,128)} custom-call(f32[1024,128]{1,0:T(8,128)S(1)} %bitcast.13, f32[2048,128]{1,0:T(8,128)S(1)} %bitcast.12, f32[4,720,128]{2,1,0:T(8,128)} %bitcast.15, f32[4,90,8,128]{3,2,1,0:T(8,128)} %get-tuple-element.31.east_hbm, f32[4,90,8,128]{3,2,1,0:T(8,128)} %get-tuple-element.32.north_hbm), custom_call_target="tpu_custom_call" | custom-call | flops 47185920 | bytes 4423680 | tf_op jit(solution)/shard_map/pallas_call | solution.py:360
  (3 shorter events, 0.1 us)
Async XLA Ops:
  11.0 34.2 %all-to-all-start = ((f32[32,6,16,128]{3,2,1,0:T(8,128)}), f32[32,6,16,128]{3,2,1,0:T(8,128)S(1)}, u32[]{:S(2)}, u32[]{:S(2)}) async-start(f32[32,6,16,128]{3,2,1,0:T(8,128)} %bitcast.4), calls=%async_computation | async-start | bytes 3145728 | tf_op jit(solution)/shard_map/all_to_all | solution.py:423
  21.8 6.5 %copy-start.4 = (f32[64,64]{1,0:T(8,128)S(1)}, f32[64,64]{1,0:T(8,128)}, u32[]{:S(2)}) copy-start(f32[64,64]{1,0:T(8,128)} %filter_ref.1) | copy-start | bytes 49156
  21.8 6.4 %copy-start.5 = (s32[4,720]{1,0:T(4,128)S(1)}, s32[4,720]{1,0:T(4,128)}, u32[]{:S(2)}) copy-start(s32[4,720]{1,0:T(4,128)} %count_ref.1) | copy-start | bytes 34564
  21.8 6.4 %copy-start.6 = (s32[4,720]{1,0:T(4,128)S(1)}, s32[4,720]{1,0:T(4,128)}, u32[]{:S(2)}) copy-start(s32[4,720]{1,0:T(4,128)} %kind_ref.1) | copy-start | bytes 34564
  21.8 6.4 %copy-start.7 = (f32[8,192]{1,0:T(8,128)S(1)}, f32[8,192]{1,0:T(8,128)}, u32[]{:S(2)}) copy-start(f32[8,192]{1,0:T(8,128)} %table_ref.1) | copy-start | bytes 18436
  26.1 2.1 %copy-start = (f32[6,6,256,128]{3,2,1,0:T(8,128)}, f32[6,6,256,128]{3,2,1,0:T(8,128)S(1)}, u32[]{:S(2)}) copy-start(f32[6,6,256,128]{3,2,1,0:T(8,128)S(1)} %shard_map.75.perturb_hbm) | copy-start | bytes 14155780
  31.3 0.8 copy-start.2
  47.7 5.0 %collective-permute-start.6 = (f32[384,384]{1,0:T(8,128)S(1)}, f32[384,384]{1,0:T(8,128)S(1)}, u32[]{:S(2)}, u32[]{:S(2)}) collective-permute-start(f32[384,384]{1,0:T(8,128)S(1)} %get-tuple-element.30), channel_id=1, source_target_pairs={{0,32},{32,0},{64,96},{96,64},{1,33},{33,1},{65,97},{97,65},{2,34}... | collective-permute-start | bytes 1769480 | tf_op jit(solution)/shard_map/ppermute | solution.py:470
  49.6 14.0 %copy-start.3 = (f32[384,256]{1,0:T(8,128)S(1)}, f32[384,256]{1,0:T(8,128)}, u32[]{:S(2)}) copy-start(f32[384,256]{1,0:T(8,128)} %copy-done.2) | copy-start | bytes 1179652
  49.6 1.9 %collective-permute-start = (f32[384,256]{1,0:T(8,128)S(1)}, f32[384,256]{1,0:T(8,128)S(1)}, u32[]{:S(2)}, u32[]{:S(2)}) collective-permute-start(f32[384,256]{1,0:T(8,128)S(1)} %get-tuple-element.24), channel_id=1, source_target_pairs={{0,32},{32,0},{64,96},{96,64},{1,33},{33,1},{65,97},{97,65},{2,34}... | collective-permute-start | bytes 1179656 | tf_op jit(solution)/shard_map/ppermute | solution.py:470
  51.6 12.1 %collective-permute-start.1 = (f32[384,256]{1,0:T(8,128)S(1)}, f32[384,256]{1,0:T(8,128)S(1)}, u32[]{:S(2)}, u32[]{:S(2)}) collective-permute-start(f32[384,256]{1,0:T(8,128)S(1)} %shard_map.77.on_chip_ref), channel_id=1, source_target_pairs={{0,64},{32,96},{64,0},{96,32},{1,65},{33,97},{65,1},{97,33},{2,66}... | collective-permute-start | bytes 1179656 | tf_op jit(solution)/shard_map/ppermute | solution.py:472
  52.8 22.9 %collective-permute-start.7 = (f32[384,384]{1,0:T(8,128)S(1)}, f32[384,384]{1,0:T(8,128)S(1)}, u32[]{:S(2)}, u32[]{:S(2)}) collective-permute-start(f32[384,384]{1,0:T(8,128)S(1)} %shard_map.84.on_chip_ref), channel_id=1, source_target_pairs={{0,64},{32,96},{64,0},{96,32},{1,65},{33,97},{65,1},{97,33},{2,66}... | collective-permute-start | bytes 1769480 | tf_op jit(solution)/shard_map/ppermute | solution.py:472
  63.7 12.3 %collective-permute-start.2 = (f32[384,256]{1,0:T(8,128)S(1)}, f32[384,256]{1,0:T(8,128)S(1)}, u32[]{:S(2)}, u32[]{:S(2)}) collective-permute-start(f32[384,256]{1,0:T(8,128)S(1)} %shard_map.78.own_ref), channel_id=1, source_target_pairs={{0,32},{32,0},{64,96},{96,64},{1,33},{33,1},{65,97},{97,65},{2,34}... | collective-permute-start | bytes 1179656 | tf_op jit(solution)/shard_map/ppermute | solution.py:474
  75.8 21.1 %collective-permute-start.8 = (f32[384,384]{1,0:T(8,128)S(1)}, f32[384,384]{1,0:T(8,128)}, u32[]{:S(2)}, u32[]{:S(2)}) collective-permute-start(f32[384,384]{1,0:T(8,128)S(1)} %shard_map.85.own_ref), channel_id=1, source_target_pairs={{0,32},{32,0},{64,96},{96,64},{1,33},{33,1},{65,97},{97,65},{2,34}... | collective-permute-start | bytes 1769480 | tf_op jit(solution)/shard_map/ppermute | solution.py:474
  78.5 0.8 copy-start.1
  79.3 23.1 %all-to-all-start.1 = ((f32[32,2,16,128]{3,2,1,0:T(8,128)}), f32[32,2,16,128]{3,2,1,0:T(8,128)S(1)}, u32[]{:S(2)}, u32[]{:S(2)}) async-start(f32[32,2,16,128]{3,2,1,0:T(8,128)} %copy-done.1), calls=%async_computation.1 | async-start | bytes 1048576 | tf_op jit(solution)/shard_map/all_to_all | solution.py:423
  86.0 1.4 %collective-permute-start.3 = (f32[80,384]{1,0:T(8,128)S(1)}, f32[80,384]{1,0:T(8,128)S(1)}, u32[]{:S(2)}, u32[]{:S(2)}) collective-permute-start(f32[80,384]{1,0:T(8,128)S(1)} %get-tuple-element.27), channel_id=1, source_target_pairs={{0,32},{32,0},{64,96},{96,64},{1,33},{33,1},{65,97},{97,65},{2,34}... | collective-permute-start | bytes 368648 | tf_op jit(solution)/shard_map/ppermute | solution.py:470
  87.5 9.3 %collective-permute-start.4 = (f32[80,384]{1,0:T(8,128)S(1)}, f32[80,384]{1,0:T(8,128)S(1)}, u32[]{:S(2)}, u32[]{:S(2)}) collective-permute-start(f32[80,384]{1,0:T(8,128)S(1)} %shard_map.81.on_chip_ref), channel_id=1, source_target_pairs={{0,64},{32,96},{64,0},{96,32},{1,65},{33,97},{65,1},{97,33},{2,66}... | collective-permute-start | bytes 368648 | tf_op jit(solution)/shard_map/ppermute | solution.py:472
  96.8 4.0 %collective-permute-start.5 = (f32[80,384]{1,0:T(8,128)S(1)}, f32[80,384]{1,0:T(8,128)S(1)}, u32[]{:S(2)}, u32[]{:S(2)}) collective-permute-start(f32[80,384]{1,0:T(8,128)S(1)} %shard_map.82.own_ref), channel_id=1, source_target_pairs={{0,32},{32,0},{64,96},{96,64},{1,33},{33,1},{65,97},{97,65},{2,34}... | collective-permute-start | bytes 368648 | tf_op jit(solution)/shard_map/ppermute | solution.py:474

commit v2 on v1

--- a/solution.py
+++ b/solution.py
@@ -9,7 +9,7 @@
 
 
 ITERS = 16
-UNROLL = 4
+UNROLL = 8
 SUB = 8
 LANES = 128
 VMEM = pl.BlockSpec(memory_space=pltpu.VMEM)
@@ -96,14 +96,14 @@
 
 
 def spread_out(
-    control_hbm, diff_hbm, sent_ref, east_hbm, north_hbm,
-    diffusivity, control, east, north, field, turned, flat, staged, sems,
+    control_hbm, diff_hbm, sent_hbm, east_hbm, north_hbm,
+    diffusivity, ready, control, east, north, field, turned, flat, staged, sems,
 ):
     planes, lon, lat = control.shape
     rows, steps = field.shape[:2]
     blocks = lat // rows
     tiles = turned.shape[0]
-    height = tiles * planes * rows
+    height = planes * rows
     pitch = staged.shape[0] // blocks
     fetch_diff = pltpu.make_async_copy(diff_hbm, diffusivity, sems.at[0])
     fetch_diff.start()
@@ -136,13 +136,23 @@
     for i in range(rows):
         for r in range(steps):
             flat[i, pl.ds(r, SUB, stride=steps), :] = field[i, r]
-        for start, width in blocks_of(lon):
-            block = flat[i, start : start + LANES, :].T
+    stores = []
+    for tile in range(tiles):
+        for i in range(rows):
+            block = flat[i, tile * LANES : (tile + 1) * LANES, :].T
             for q in range(planes):
-                row = (start // LANES * planes + q) * rows + i
-                staged[pl.ds(row, blocks, stride=pitch), :] = block[q * blocks : (q + 1) * blocks, :]
-    for b in range(blocks):
-        sent_ref[height * b : height * (b + 1), :] = staged[pitch * b : pitch * b + height, :]
+                staged[pl.ds((tile * planes + q) * rows + i, blocks, stride=pitch), :] = block[
+                    q * blocks : (q + 1) * blocks, :
+                ]
+        for b in range(blocks):
+            start = pitch * b + height * tile
+            ready[tile, b] = staged[start : start + height, :]
+        stores.append(
+            pltpu.make_async_copy(ready.at[tile], sent_hbm.at[:, tile], sems.at[4 + tile])
+        )
+        stores[-1].start()
+    for store in stores:
+        store.wait()
     keep_east.wait()
     keep_north.wait()
 
@@ -306,16 +316,23 @@
                     out_ref[:, v * half : (v + 1) * half] = block[: out_ref.shape[0], :]
 
 
-def lift(first, place, core_ref, band_ref, own_ref, other_ref, perturb_hbm, *rest):
-    out_ref, perturb, adjoint, parts, sems = rest[-5:]
+def lift(
+    first, place, fetched, ahead, core_ref, band_ref, own_ref, other_ref, perturb_ref, *rest
+):
+    *rest, adjoint, parts, sems = rest
+    perturb = perturb_ref if fetched else rest.pop()
     count, products, flat = perturb.shape[:3]
+    copies = [] if fetched else fetch_tiles(first, perturb_ref, perturb, sems)
+    if ahead:
+        tail = pltpu.make_async_copy(perturb_ref.at[first + count], rest.pop().at[0], sems.at[count])
+        tail.start()
+    *earlier, out_ref = rest
     members = adjoint.shape[1] // LANES
     variables = products // members
     piece = out_ref.shape[2] // members
     core = core_ref[0]
     half = flat // 2
-    copies = fetch_tiles(first, perturb_hbm, perturb, sems)
-    for earlier_ref in rest[:-5]:
+    for earlier_ref in earlier:
         out_ref[:, :place] = earlier_ref[...]
     sides = [own_ref, other_ref]
     if own_ref.shape[0] < variables * half:
@@ -326,7 +343,8 @@
                 parts[side, v * half : (v + 1) * half, :] = block.T
         sides = [parts.at[0], parts.at[1]]
     for u in range(count):
-        copies[u].wait()
+        if copies:
+            copies[u].wait()
         for side, weighted in enumerate(sides):
             base = (core if side == 0 else 1 - core) * half
             for t in range(half // SUB):
@@ -345,6 +363,8 @@
             out_ref[:, place + u, piece * k : piece * k + piece, :] = whole[
                 :, LANES * k : LANES * (k + 1)
             ].reshape(-1, piece, LANES)
+    if ahead:
+        tail.wait()
 
 
 def add_up(keep_ref, got_ref, out_ref):
@@ -409,12 +429,17 @@
 
     sent, east, north = call(
         spread_out,
-        [f32(devices * tiles * height, LANES), resting, resting],
+        [pltpu.HBM((devices, tiles, height, LANES), jnp.float32), resting, resting],
         work,
         2 * size,
         [HBM, HBM],
-        [VMEM, HBM, HBM],
-        [pltpu.VMEM((lon, lat), jnp.float32), *vmem, pltpu.SemaphoreType.DMA((4,))],
+        [HBM] * 3,
+        [
+            pltpu.VMEM((lon, lat), jnp.float32),
+            pltpu.VMEM((tiles, devices, height, LANES), jnp.float32),
+            *vmem,
+            pltpu.SemaphoreType.DMA((4 + tiles,)),
+        ],
         20,
     )(control_t, pltpu.with_memory_space_constraint(diff_t, pltpu.HBM))
     east, north = (pltpu.with_memory_space_constraint(e, pltpu.HBM) for e in (east, north))
@@ -452,20 +477,22 @@
     lifted = []
     for h, (first, count) in enumerate(chunks):
         part = parts[h]
+        room = (count, members * variables, flat, LANES)
         scratch = [
-            pltpu.VMEM((count, members * variables, flat, LANES), jnp.float32),
+            pltpu.VMEM(room, jnp.float32),
             pltpu.VMEM((flat, members * LANES), jnp.float32),
             pltpu.VMEM((2, variables * half, LANES), jnp.float32),
-            pltpu.SemaphoreType.DMA((count,)),
+            pltpu.SemaphoreType.DMA((count + 1,)),
         ]
-        send, keep = call(
+        keeps = h == 0
+        send, keep, *tiles_here = call(
             functools.partial(partial_sums, first),
-            [part, part],
+            [part, part] + ([pltpu.VMEM(room, jnp.float32)] if keeps else []),
             count << 28,
             count * size,
             [SMEM, VMEM, VMEM, HBM],
             None,
-            scratch,
+            scratch[1:] if keeps else scratch,
         )(core, band, pieces, perturb)
         got = lax.ppermute(send, "mem", other_core)
         on_chip = call(add_up, part, 1 << 18, size)(keep, got)
@@ -476,15 +503,19 @@
         place = first - start
         begins = place == 0
 
-        home = call(
-            functools.partial(lift, first, place),
-            f32(devices, place + count, height, LANES),
+        fetched, ahead = h != 1, h == 1
+        rows_here = tiles_here[0] if keeps else tail if fetched else perturb
+        tile_room = pltpu.VMEM((1, *room[1:]), jnp.float32)
+        home, *tails = call(
+            functools.partial(lift, first, place, fetched, ahead),
+            [f32(devices, place + count, height, LANES)] + ([tile_room] if ahead else []),
             count << 28,
             count * size,
-            [SMEM, VMEM, VMEM, VMEM, HBM] + ([] if begins else [VMEM]),
+            [SMEM, VMEM, VMEM, VMEM, VMEM if fetched else HBM] + ([] if begins else [VMEM]),
             None,
-            scratch,
-        )(core, band_t, own, other, perturb, *([] if begins else [home]))
+            scratch[1:] if fetched else scratch,
+        )(core, band_t, own, other, rows_here, *([] if begins else [home]))
+        tail = tails[0] if tails else None
         if first + count == start + total:
             lifted.append(exchange(home).reshape(-1, LANES))
 

time: 140 us -> 137 us (0.979)
  Pallas kernels: 42.4 us -> 39.5 us
    pallas_call x16, Pallas kernels: 42.4 us -> 39.5 us  [run(): pl.pallas_call(kernel, out_shape=out_shape, in_specs=ins or [VMEM] * len(...]
  transfers between devices with their start and end apart: 11 -> 11, of which waited for: 6 -> 6; matrix products, arithmetic and copies ran while one was open for 0% -> 0% of each run, Pallas kernels for 13% -> 12%
where the time goes in v2:
time: 137 us; the launch traced here: 136 us
  waiting for transfers between devices  45.3 us (33%)
  Pallas kernels  39.5 us (29%)
  blocking collectives  26.5 us (19%)
  starting transfers between devices  20.7 us (15%)
  local copies, waits for them, and re-layouts  3.77 us (3%)
    pallas_call x16, Pallas kernels, run(): pl.pallas_call(kernel, out_shape=out_shape, in_specs=ins or [VMEM] * len(...  39.5 us
    ppermute x3, waiting for transfers between devices, local(): got = lax.ppermute(on_chip, 'mem', next_chip)  29.7 us
    all_to_all x1, blocking collectives, exchange(): lax.all_to_all(sent.reshape(devices, -1, height, LANES), 'wide', 0, 0, ti...  26.5 us
    all_to_all x2, starting transfers between devices, exchange(): lax.all_to_all(sent.reshape(devices, -1, height, LANES), 'wide', 0, 0, ti...  16 us
    all_to_all x2, waiting for transfers between devices, exchange(): lax.all_to_all(sent.reshape(devices, -1, height, LANES), 'wide', 0, 0, ti...  13.1 us
    unnamed x16, local copies, waits for them, and re-layouts  3.77 us
    ppermute x3, starting transfers between devices, local(): got = lax.ppermute(on_chip, 'mem', next_chip)  3.46 us
  transfers between devices with their start and end apart: 11, of which 6 were waited for; matrix products, arithmetic and copies ran while one was open for 0% of the time, Pallas kernels for 12%

profile of v2, /device:TPU:0, one launch (start us, length us, event | category | flops | bytes accessed | tf_op | source)
XLA Modules:
  0.0 136.1 jit_solution(10632470635610758741)
XLA Ops:
  0.0 10.6 %shard_map.74 = (f32[32,6,16,128]{3,2,1,0:T(8,128)}, f32[4,90,8,128]{3,2,1,0:T(8,128)}, f32[4,90,8,128]{3,2,1,0:T(8,128)}) custom-call(f32[4,720,128]{2,1,0:T(8,128)} %bitcast.13, f32[720,128]{1,0:T(8,128)} %bitcast.16), custom_call_target="tpu_custom_call" | custom-call | flops 47185920 | bytes 2949120 | tf_op jit(solution)/shard_map/pallas_call | solution.py:380
  10.6 10.8 %all-to-all-start = ((f32[32,6,16,128]{3,2,1,0:T(8,128)}), f32[32,6,16,128]{3,2,1,0:T(8,128)S(1)}, u32[]{:S(2)}, u32[]{:S(2)}) async-start(f32[32,6,16,128]{3,2,1,0:T(8,128)} %get-tuple-element.25), calls=%async_computation | async-start | bytes 3145728 | tf_op jit(solution)/shard_map/all_to_all | solution.py:448
  21.4 0.0 copy-start.4
  21.4 0.0 copy-start.5
  21.4 0.0 copy-start.6
  21.4 0.0 copy-start.7
  21.4 4.3 %shard_map.75.perturb_hbm.perturb_ref = f32[6,6,256,128]{3,2,1,0:T(8,128)S(1)} custom-call(f32[6,64,4,720]{3,2,1,0:T(4,128)} %bitcast.15), custom_call_target="tpu_custom_call" | custom-call | flops 1048576 | bytes 8847360 | tf_op jit(solution)/shard_map/pallas_call | solution.py:380
  25.7 0.0 copy-start
  25.7 2.1 %copy-done = f32[6,6,256,128]{3,2,1,0:T(8,128)} copy-done((f32[6,6,256,128]{3,2,1,0:T(8,128)}, f32[6,6,256,128]{3,2,1,0:T(8,128)S(1)}, u32[]{:S(2)}) %copy-start) | copy-done | bytes 4718616
  27.8 0.0 copy-done.4
  27.8 0.0 copy-done.5
  27.8 0.0 copy-done.6
  27.8 0.0 copy-done.7
  27.8 3.0 %shard_map.73 = (f32[256,256]{1,0:T(8,128)S(1)}, f32[256,256]{1,0:T(8,128)S(1)}, f32[384,256]{1,0:T(8,128)S(1)}, f32[384,384]{1,0:T(8,128)S(1)}, f32[80,384]{1,0:T(8,128)S(1)}) custom-call(s32[1]{0:T(128)} %bitcast.core_ref, f32[64,64]{1,0:T(8,128)S(1)} %copy-done.4, f32[8,192]{1,0:T(8,128)S(1)} %copy-done.7, s32[4,720]{1,0:T(4,128)S(1)} %copy-done.5, ...), custom_call_target="tpu_custom_call" | custom-call | flops 268435456 | bytes 4194304 | tf_op jit(solution)/shard_map/pallas_call | solution.py:380
  30.9 0.0 copy-start.2
  30.9 0.8 copy-done.2
  31.7 13.1 %all-to-all-done.pieces_ref = f32[32,6,16,128]{3,2,1,0:T(8,128)S(1)} async-done(((f32[32,6,16,128]{3,2,1,0:T(8,128)}), f32[32,6,16,128]{3,2,1,0:T(8,128)S(1)}, u32[]{:S(2)}, u32[]{:S(2)}) %all-to-all-start) | async-done | bytes 1572896 | tf_op jit(solution)/shard_map/all_to_all | solution.py:448
  44.8 2.5 %shard_map.83 = (f32[384,384]{1,0:T(8,128)S(1)}, f32[384,384]{1,0:T(8,128)S(1)}) custom-call(s32[1]{0:T(128)} %bitcast.core_ref, f32[256,256]{1,0:T(8,128)S(1)} %get-tuple-element.24.band_ref, f32[32,6,16,128]{3,2,1,0:T(8,128)S(1)} %all-to-all-done.pieces_ref, f32[6,6,256,128]{3,2,1,0:T(8,128)} %copy-done), custom_call_target="tpu_custom_call" | custom-call | flops 805306368 | bytes 4423680 | tf_op jit(solution)/shard_map/pallas_call | solution.py:380
  47.3 0.1 collective-permute-start.6
  47.4 1.8 %shard_map.76 = (f32[384,256]{1,0:T(8,128)S(1)}, f32[384,256]{1,0:T(8,128)S(1)}, f32[2,6,256,128]{3,2,1,0:T(8,128)S(1)}) custom-call(s32[1]{0:T(128)} %bitcast.core_ref, f32[256,256]{1,0:T(8,128)S(1)} %get-tuple-element.24.band_ref, f32[32,6,16,128]{3,2,1,0:T(8,128)S(1)} %all-to-all-done.pieces_ref, f32[6,6,256,128]{3,2,1,0:T(8,128)} %copy-done), custom_call_target="tpu_custom_call" | custom-call | flops 536870912 | bytes 2949120 | tf_op jit(solution)/shard_map/pallas_call | solution.py:380
  49.2 0.6 collective-permute-start
  49.8 1.3 collective-permute-done.got_ref
  51.2 1.1 collective-permute-start.1
  52.3 0.0 collective-permute-done.6.got_ref
  52.3 0.0 copy-start.3
  52.3 0.1 shard_map.84.on_chip_ref
  52.4 1.3 collective-permute-start.7
  53.6 9.6 %collective-permute-done.1.got_ref = f32[384,256]{1,0:T(8,128)S(1)} collective-permute-done((f32[384,256]{1,0:T(8,128)S(1)}, f32[384,256]{1,0:T(8,128)S(1)}, u32[]{:S(2)}, u32[]{:S(2)}) %collective-permute-start.1) | collective-permute-done | bytes 393248 | tf_op jit(solution)/shard_map/ppermute | solution.py:499
  63.3 0.1 shard_map.78.own_ref
  63.3 0.1 collective-permute-start.2
  63.4 11.9 %collective-permute-done.7.got_ref = f32[384,384]{1,0:T(8,128)S(1)} collective-permute-done((f32[384,384]{1,0:T(8,128)S(1)}, f32[384,384]{1,0:T(8,128)S(1)}, u32[]{:S(2)}, u32[]{:S(2)}) %collective-permute-start.7) | collective-permute-done | bytes 589856 | tf_op jit(solution)/shard_map/ppermute | solution.py:499
  75.3 0.0 copy-done.3
  75.3 0.1 shard_map.85.own_ref
  75.4 0.1 collective-permute-start.8
  75.5 0.0 collective-permute-done.2.other_ref
  75.5 0.8 shard_map.79
  76.3 0.0 copy-start.1
  76.3 0.8 copy-done.1
  77.1 5.3 %all-to-all-start.1 = ((f32[32,2,16,128]{3,2,1,0:T(8,128)}), f32[32,2,16,128]{3,2,1,0:T(8,128)S(1)}, u32[]{:S(2)}, u32[]{:S(2)}) async-start(f32[32,2,16,128]{3,2,1,0:T(8,128)} %copy-done.1), calls=%async_computation.1 | async-start | bytes 1048576 | tf_op jit(solution)/shard_map/all_to_all | solution.py:448
  82.4 1.4 %shard_map.80 = (f32[80,384]{1,0:T(8,128)S(1)}, f32[80,384]{1,0:T(8,128)S(1)}) custom-call(s32[1]{0:T(128)} %bitcast.core_ref, f32[256,256]{1,0:T(8,128)S(1)} %get-tuple-element.24.band_ref, f32[32,6,16,128]{3,2,1,0:T(8,128)S(1)} %all-to-all-done.pieces_ref, f32[6,6,256,128]{3,2,1,0:T(8,128)} %copy-done), custom_call_target="tpu_custom_call" | custom-call | flops 268435456 | bytes 1474560 | tf_op jit(solution)/shard_map/pallas_call | solution.py:380
  83.9 0.3 collective-permute-start.3
  84.1 1.1 collective-permute-done.3.got_ref
  85.3 1.1 collective-permute-start.4
  86.4 8.2 %collective-permute-done.4.got_ref = f32[80,384]{1,0:T(8,128)S(1)} collective-permute-done((f32[80,384]{1,0:T(8,128)S(1)}, f32[80,384]{1,0:T(8,128)S(1)}, u32[]{:S(2)}, u32[]{:S(2)}) %collective-permute-start.4) | collective-permute-done | bytes 122912 | tf_op jit(solution)/shard_map/ppermute | solution.py:499
  94.6 0.1 collective-permute-start.5
  94.7 0.0 collective-permute-done.8.other_ref
  94.7 4.0 %shard_map.86 = (f32[32,3,16,128]{3,2,1,0:T(8,128)S(1)}, f32[1,6,256,128]{3,2,1,0:T(8,128)S(1)}) custom-call(s32[1]{0:T(128)} %bitcast.core_ref, f32[256,256]{1,0:T(8,128)S(1)} %get-tuple-element.22.band_ref, f32[384,384]{1,0:T(8,128)S(1)} %shard_map.85.own_ref, f32[384,384]{1,0:T(8,128)} %collective-permute-done.8.other_ref, f32[6,6,256,128]{3,2,1,0:T(8,128)} %copy-done), custom_call_target="tpu_custom_call" | custom-call | flops 805306368 | bytes 4423680 | tf_op jit(solution)/shard_map/pallas_call | solution.py:380
  98.7 0.0 collective-permute-done.5.other_ref
  98.7 0.6 shard_map.87
  99.3 0.0 all-to-all-done.1
  99.3 26.5 %all_to_all.15 = f32[32,4,16,128]{3,2,1,0:T(8,128)S(1)} all-to-all(f32[32,4,16,128]{3,2,1,0:T(8,128)S(1)} %shard_map.87), channel_id=1, replica_groups=mesh['mem'=4,'wide'=32] {'wide'}, dimensions={0} | all-to-all | bytes 2097152 | tf_op jit(solution)/shard_map/all_to_all | solution.py:448
  125.8 10.1 %shard_map.88 = f32[4,720,128]{2,1,0:T(8,128)} custom-call(f32[1024,128]{1,0:T(8,128)S(1)} %bitcast.12, f32[2048,128]{1,0:T(8,128)S(1)} %bitcast.11, f32[4,720,128]{2,1,0:T(8,128)} %bitcast.14, f32[4,90,8,128]{3,2,1,0:T(8,128)} %get-tuple-element.37.east_hbm, f32[4,90,8,128]{3,2,1,0:T(8,128)} %get-tuple-element.38.north_hbm), custom_call_target="tpu_custom_call" | custom-call | flops 47185920 | bytes 4423680 | tf_op jit(solution)/shard_map/pallas_call | solution.py:380
  (3 shorter events, 0.1 us)
Async XLA Ops:
  10.6 34.2 %all-to-all-start = ((f32[32,6,16,128]{3,2,1,0:T(8,128)}), f32[32,6,16,128]{3,2,1,0:T(8,128)S(1)}, u32[]{:S(2)}, u32[]{:S(2)}) async-start(f32[32,6,16,128]{3,2,1,0:T(8,128)} %get-tuple-element.25), calls=%async_computation | async-start | bytes 3145728 | tf_op jit(solution)/shard_map/all_to_all | solution.py:448
  21.4 6.5 %copy-start.4 = (f32[64,64]{1,0:T(8,128)S(1)}, f32[64,64]{1,0:T(8,128)}, u32[]{:S(2)}) copy-start(f32[64,64]{1,0:T(8,128)} %filter_ref.1) | copy-start | bytes 49156
  21.4 6.4 %copy-start.5 = (s32[4,720]{1,0:T(4,128)S(1)}, s32[4,720]{1,0:T(4,128)}, u32[]{:S(2)}) copy-start(s32[4,720]{1,0:T(4,128)} %count_ref.1) | copy-start | bytes 34564
  21.4 6.4 %copy-start.6 = (s32[4,720]{1,0:T(4,128)S(1)}, s32[4,720]{1,0:T(4,128)}, u32[]{:S(2)}) copy-start(s32[4,720]{1,0:T(4,128)} %kind_ref.1) | copy-start | bytes 34564
  21.4 6.4 %copy-start.7 = (f32[8,192]{1,0:T(8,128)S(1)}, f32[8,192]{1,0:T(8,128)}, u32[]{:S(2)}) copy-start(f32[8,192]{1,0:T(8,128)} %table_ref.1) | copy-start | bytes 18436
  25.7 2.1 %copy-start = (f32[6,6,256,128]{3,2,1,0:T(8,128)}, f32[6,6,256,128]{3,2,1,0:T(8,128)S(1)}, u32[]{:S(2)}) copy-start(f32[6,6,256,128]{3,2,1,0:T(8,128)S(1)} %shard_map.75.perturb_hbm.perturb_ref) | copy-start | bytes 14155780
  30.9 0.8 copy-start.2
  47.3 5.0 %collective-permute-start.6 = (f32[384,384]{1,0:T(8,128)S(1)}, f32[384,384]{1,0:T(8,128)S(1)}, u32[]{:S(2)}, u32[]{:S(2)}) collective-permute-start(f32[384,384]{1,0:T(8,128)S(1)} %get-tuple-element.34), channel_id=1, source_target_pairs={{0,32},{32,0},{64,96},{96,64},{1,33},{33,1},{65,97},{97,65},{2,34}... | collective-permute-start | bytes 1769480 | tf_op jit(solution)/shard_map/ppermute | solution.py:497
  49.2 1.9 %collective-permute-start = (f32[384,256]{1,0:T(8,128)S(1)}, f32[384,256]{1,0:T(8,128)S(1)}, u32[]{:S(2)}, u32[]{:S(2)}) collective-permute-start(f32[384,256]{1,0:T(8,128)S(1)} %get-tuple-element.27), channel_id=1, source_target_pairs={{0,32},{32,0},{64,96},{96,64},{1,33},{33,1},{65,97},{97,65},{2,34}... | collective-permute-start | bytes 1179656 | tf_op jit(solution)/shard_map/ppermute | solution.py:497
  51.2 12.1 %collective-permute-start.1 = (f32[384,256]{1,0:T(8,128)S(1)}, f32[384,256]{1,0:T(8,128)S(1)}, u32[]{:S(2)}, u32[]{:S(2)}) collective-permute-start(f32[384,256]{1,0:T(8,128)S(1)} %shard_map.77.on_chip_ref), channel_id=1, source_target_pairs={{0,64},{32,96},{64,0},{96,32},{1,65},{33,97},{65,1},{97,33},{2,66}... | collective-permute-start | bytes 1179656 | tf_op jit(solution)/shard_map/ppermute | solution.py:499
  52.3 23.0 %copy-start.3 = (f32[384,384]{1,0:T(8,128)S(1)}, f32[384,384]{1,0:T(8,128)}, u32[]{:S(2)}) copy-start(f32[384,384]{1,0:T(8,128)} %copy-done.2) | copy-start | bytes 1769476
  52.4 22.9 %collective-permute-start.7 = (f32[384,384]{1,0:T(8,128)S(1)}, f32[384,384]{1,0:T(8,128)S(1)}, u32[]{:S(2)}, u32[]{:S(2)}) collective-permute-start(f32[384,384]{1,0:T(8,128)S(1)} %shard_map.84.on_chip_ref), channel_id=1, source_target_pairs={{0,64},{32,96},{64,0},{96,32},{1,65},{33,97},{65,1},{97,33},{2,66}... | collective-permute-start | bytes 1769480 | tf_op jit(solution)/shard_map/ppermute | solution.py:499
  63.3 12.1 %collective-permute-start.2 = (f32[384,256]{1,0:T(8,128)S(1)}, f32[384,256]{1,0:T(8,128)S(1)}, u32[]{:S(2)}, u32[]{:S(2)}) collective-permute-start(f32[384,256]{1,0:T(8,128)S(1)} %shard_map.78.own_ref), channel_id=1, source_target_pairs={{0,32},{32,0},{64,96},{96,64},{1,33},{33,1},{65,97},{97,65},{2,34}... | collective-permute-start | bytes 1179656 | tf_op jit(solution)/shard_map/ppermute | solution.py:501
  75.4 19.3 %collective-permute-start.8 = (f32[384,384]{1,0:T(8,128)S(1)}, f32[384,384]{1,0:T(8,128)}, u32[]{:S(2)}, u32[]{:S(2)}) collective-permute-start(f32[384,384]{1,0:T(8,128)S(1)} %shard_map.85.own_ref), channel_id=1, source_target_pairs={{0,32},{32,0},{64,96},{96,64},{1,33},{33,1},{65,97},{97,65},{2,34}... | collective-permute-start | bytes 1769480 | tf_op jit(solution)/shard_map/ppermute | solution.py:501
  76.3 0.8 copy-start.1
  77.1 22.2 %all-to-all-start.1 = ((f32[32,2,16,128]{3,2,1,0:T(8,128)}), f32[32,2,16,128]{3,2,1,0:T(8,128)S(1)}, u32[]{:S(2)}, u32[]{:S(2)}) async-start(f32[32,2,16,128]{3,2,1,0:T(8,128)} %copy-done.1), calls=%async_computation.1 | async-start | bytes 1048576 | tf_op jit(solution)/shard_map/all_to_all | solution.py:448
  83.9 1.4 %collective-permute-start.3 = (f32[80,384]{1,0:T(8,128)S(1)}, f32[80,384]{1,0:T(8,128)S(1)}, u32[]{:S(2)}, u32[]{:S(2)}) collective-permute-start(f32[80,384]{1,0:T(8,128)S(1)} %get-tuple-element.31), channel_id=1, source_target_pairs={{0,32},{32,0},{64,96},{96,64},{1,33},{33,1},{65,97},{97,65},{2,34}... | collective-permute-start | bytes 368648 | tf_op jit(solution)/shard_map/ppermute | solution.py:497
  85.3 9.3 %collective-permute-start.4 = (f32[80,384]{1,0:T(8,128)S(1)}, f32[80,384]{1,0:T(8,128)S(1)}, u32[]{:S(2)}, u32[]{:S(2)}) collective-permute-start(f32[80,384]{1,0:T(8,128)S(1)} %shard_map.81.on_chip_ref), channel_id=1, source_target_pairs={{0,64},{32,96},{64,0},{96,32},{1,65},{33,97},{65,1},{97,33},{2,66}... | collective-permute-start | bytes 368648 | tf_op jit(solution)/shard_map/ppermute | solution.py:499
  94.6 4.1 %collective-permute-start.5 = (f32[80,384]{1,0:T(8,128)S(1)}, f32[80,384]{1,0:T(8,128)S(1)}, u32[]{:S(2)}, u32[]{:S(2)}) collective-permute-start(f32[80,384]{1,0:T(8,128)S(1)} %shard_map.82.own_ref), channel_id=1, source_target_pairs={{0,32},{32,0},{64,96},{96,64},{1,33},{33,1},{65,97},{97,65},{2,34}... | collective-permute-start | bytes 368648 | tf_op jit(solution)/shard_map/ppermute | solution.py:501
